TPU v7x, 32 devices: a whole 2x2x4 slice. The times are simulated.
32 devices in a mesh: gx: 4 (over y, x), gy: 8 (over z, core).
Axes of the slice: x: 2, y: 2, z: 4, core: 2. Of those that a mesh axis runs over, the one named last changes fastest.
Arguments:
- schur: float32 [4, 8, 512, 512], P('gx', 'gy'), may hold values from -1 to 25, as said below
- precond: float32 [4, 8, 512, 512], P('gx', 'gy'), may hold values from -1 to 25, as said below
- loads: float32 [4, 8, 512, 256], P('gx', 'gy'), may hold values from -12 to 12
- coarse_inv: float32 [128, 128], P('gx'), may hold values from -1 to 25, as said below
- edge_rows: int32 [4, 8, 512], P('gx', 'gy'), may hold values from 0 to 511, each once within a row
- corner_rows: int32 [4, 8, 4], P('gx', 'gy'), may hold values from 0 to 511, as said below
Outputs:
- multipliers: float32 [4, 8, 512, 256], P('gx', 'gy')
- residual: float32 [4, 8, 512, 256], P('gx', 'gy')
Inputs may be any that keep to these rules, and one draw needn't show every extreme that they name: `edge_rows`: for every subdomain the 512 entries name each local interface row once. `corner_rows`: local interface rows of each subdomain's 4 corner modes; entries of one subdomain may repeat. `schur`: every subdomain's block is symmetric positive definite. `precond`: every subdomain's block is symmetric positive definite. `coarse_inv`: symmetric positive definite; row and column (i * 8 + j) * 4 + m belong to mode m of subdomain (i, j).
All inputs are finite; a program needn't handle non-finite values.
Results may differ from a plain program's by a relative error of at most 0.00017.
Values sent between devices are 32-bit elements; how exact they have to be, the bound alone decides.
No kernel may reach another device: no remote copies, remote signals or barrier semaphores. Data moves between devices by JAX's collectives and lax.ppermute only.
A program may use at most 64 MiB of HBM per device.

v0:
```python
import jax
import jax.numpy as jnp
from jax import lax
from jax.sharding import PartitionSpec as P

MODES = 4
ITERS = 2
highest = lax.Precision.HIGHEST


def with_halo(cells, sides, width):
    for axis, dim in sides:
        count = lax.axis_size(axis)
        head = lax.slice_in_dim(cells, 0, width, axis=dim)
        tail = lax.slice_in_dim(cells, cells.shape[dim] - width, cells.shape[dim], axis=dim)
        cells = jnp.concatenate(
            [
                lax.ppermute(tail, axis, [(i, (i + 1) % count) for i in range(count)]),
                cells,
                lax.ppermute(head, axis, [((i + 1) % count, i) for i in range(count)]),
            ],
            axis=dim,
        )
    return cells


def matmul(first_op, second_op):
    return jnp.dot(first_op, second_op, precision=highest, preferred_element_type=jnp.float32)


def edge_jumps(source, local_rows, inverse):
    edge_size = local_rows.shape[0] // 4
    picked = jnp.take(source, local_rows, axis=0).reshape(4, edge_size, source.shape[1])
    across = with_halo(picked[0:2], (("gx", 0),), 1)
    upward = with_halo(picked[2:4], (("gy", 0),), 1)
    west_jump = picked[0] - across[0]
    east_jump = picked[1] - across[3]
    south_jump = picked[2] - upward[0]
    north_jump = picked[3] - upward[3]
    stacked = jnp.stack([west_jump, east_jump, south_jump, north_jump]).reshape(source.shape)
    return jnp.take(stacked, inverse, axis=0)


def coarse_by_column(corner_res, coarse_inv, grid_row):
    across_count = lax.axis_size("gx")
    along_count = lax.axis_size("gy")
    column_res = lax.all_gather(corner_res, "gx", axis=0, tiled=True)
    group_rows = coarse_inv.shape[0]
    shaped = coarse_inv.reshape(group_rows, across_count, along_count, MODES)
    chosen = lax.dynamic_slice_in_dim(shaped, grid_row, 1, 2).reshape(
        group_rows, across_count * MODES
    )
    return lax.psum_scatter(matmul(chosen, column_res), "gy", scatter_dimension=0, tiled=True)


def on_device(schur, precond, loads, coarse_inv, edge_rows, corner_rows):
    schur_block = schur[0, 0]
    precond_block = precond[0, 0]
    local_loads = loads[0, 0]
    local_rows = edge_rows[0, 0]
    corner_local = corner_rows[0, 0]
    row_total = local_rows.shape[0]
    positions = jnp.arange(row_total, dtype=jnp.int32)
    inverse = jnp.zeros((row_total,), jnp.int32).at[local_rows].set(positions)
    corner_pick = (corner_local[:, None] == positions[None, :]).astype(jnp.float32)
    grid_row = lax.axis_index("gy")
    dual_rhs = edge_jumps(local_loads, local_rows, inverse)
    multipliers = jnp.zeros_like(dual_rhs)
    residual = dual_rhs
    for iteration in range(ITERS):
        corner_res = matmul(corner_pick, residual)
        coarse_sol = coarse_by_column(corner_res, coarse_inv, grid_row)
        lifted = 0.25 * matmul(precond_block, residual) + matmul(corner_pick.T, coarse_sol)
        search = edge_jumps(lifted, local_rows, inverse)
        schur_image = matmul(schur_block, search)
        numerator = lax.psum(jnp.sum(residual * search, axis=0), ("gx", "gy"))
        dual_image = edge_jumps(schur_image, local_rows, inverse)
        denominator = lax.psum(jnp.sum(search * dual_image, axis=0), ("gx", "gy"))
        step_size = numerator / denominator
        multipliers = multipliers + step_size * search
        residual = residual - step_size * dual_image
    return (multipliers[None, None], residual[None, None])


def solution(mesh):
    in_specs = (
        P("gx", "gy", None, None),
        P("gx", "gy", None, None),
        P("gx", "gy", None, None),
        P("gx", None),
        P("gx", "gy", None),
        P("gx", "gy", None),
    )
    out_specs = (P("gx", "gy", None, None), P("gx", "gy", None, None))
    return jax.shard_map(
        on_device, mesh=mesh, in_specs=in_specs, out_specs=out_specs, check_vma=False
    )
```

profile of v0, /device:TPU:10, one launch (start us, length us, event | category | flops | bytes accessed | tf_op | source)
XLA Modules:
  0.0 237.9 jit_solution(15812877509895643523)
XLA Ops:
  1.5 2.6 %gather_fusion = f32[512,256]{1,0:T(8,128)S(1)} fusion(f32[512,256]{1,0:T(8,128)} %bitcast.136, s32[1024]{0:T(1024)S(1)} %pad_clamp_fusion.1), kind=kCustom, calls=%fused_computation.clone | custom fusion | bytes 1050624 | tf_op jit(solution)/shard_map/jit(_take)/gather | solution.py:33
  5.8 1.7 collective-permute-start.3
  8.1 2.4 %scatter_custom_fusion = s32[512]{0:T(512)S(1)} fusion(s32[512]{0:T(512)S(1)} %bitcast.146, s32[512]{0:T(512)S(1)} %iota.6, s32[]{:T(128)} %constant.1.clone.1), kind=kCustom, calls=%fused_computation.90 | custom fusion | bytes 2052 | tf_op jit(solution)/shard_map/scatter | solution.py:64
  13.9 1.6 gather_fusion.1
  16.5 7.2 %all-gather = f32[4,4,256]{2,1,0:T(4,128)S(1)} all-gather(f32[1,4,256]{2,1,0:T(4,128)S(1)} %convolution_bitcast_fusion.3), channel_id=1, replica_groups=mesh['gx'=4,'gy'=8] {'gx'}, dimensions={0}, use_global_device_ids=true | all-gather | bytes 20480 | tf_op jit(solution)/shard_map/all_gather | solution.py:47
  24.0 24.0 %all-reduce = f32[32,256]{1,0:T(8,128)S(1)} all-reduce(f32[32,256]{1,0:T(8,128)S(1)} %fusion.56), channel_id=2, replica_groups=mesh['gx'=4,'gy'=8] {'gy'}, use_global_device_ids=true, to_apply=%region_1.0.clone | all-reduce | flops 8192 | bytes 65536
  48.5 2.0 fusion.2
  50.6 1.6 gather_fusion.2
  53.9 1.7 collective-permute-start.7
  58.3 3.2 %collective-permute-done.5 = f32[1,128,256]{2,1,0:T(8,128)S(1)} collective-permute-done((f32[1,128,256]{2,1,0:T(8,128)S(1)}, f32[1,128,256]{2,1,0:T(8,128)S(1)}, u32[]{:S(2)}, u32[]{:S(2)}) %collective-permute-start.5) | collective-permute-done | bytes 131104 | tf_op jit(solution)/shard_map/ppermute | solution.py:20
  61.6 1.6 gather_fusion.3
  63.2 3.2 %convolution_bitcast_fusion.1 = f32[512,256]{0,1:T(8,128)S(1)} fusion(f32[1,1,512,512]{3,2,1,0:T(8,128)} %param.8, f32[512,256]{1,0:T(8,128)S(1)} %gather_fusion.3, pred[512]{0:T(512)(128)(4,1)S(1)} %compare_and_fusion), kind=kOutput, calls=%fused_computation.18 | convolution fusion | flops 805437440 | bytes 2097664 | tf_op jit(solution)/shard_map/dot_general | solution.py:28
  66.6 1.6 gather_fusion.4
  69.5 2.1 collective-permute-start.11
  72.2 2.0 collective-permute-done.8
  74.2 3.2 %collective-permute-done.9 = f32[1,128,256]{2,1,0:T(8,128)S(1)} collective-permute-done((f32[1,128,256]{2,1,0:T(8,128)S(1)}, f32[1,128,256]{2,1,0:T(8,128)S(1)}, u32[]{:S(2)}, u32[]{:S(2)}) %collective-permute-start.9) | collective-permute-done | bytes 131104 | tf_op jit(solution)/shard_map/ppermute | solution.py:20
  77.6 1.6 gather_fusion.5
  79.4 45.9 %all-reduce.3 = (f32[256]{0:T(256)S(1)}, f32[256]{0:T(256)S(1)}) all-reduce(f32[256]{0:T(256)S(1)} %get-tuple-element.6, f32[256]{0:T(256)S(1)} %get-tuple-element.5), channel_id=1, replica_groups=mesh['gx'=4,'gy'=8] {'gx','gy'}, use_global_device_ids=true, to_apply=%region_3.5 | all-reduce | flops 512 | bytes 4096 | tf_op jit(solution)/shard_map/psum | solution.py:76
  125.7 7.8 %all-gather.1 = f32[4,4,256]{2,1,0:T(4,128)S(1)} all-gather(f32[1,4,256]{2,1,0:T(4,128)S(1)} %convolution_bitcast_fusion.2), channel_id=1, replica_groups=mesh['gx'=4,'gy'=8] {'gx'}, dimensions={0}, use_global_device_ids=true | all-gather | bytes 20480 | tf_op jit(solution)/shard_map/all_gather | solution.py:47
  133.8 21.0 %all-reduce.1 = f32[32,256]{1,0:T(8,128)S(1)} all-reduce(f32[32,256]{1,0:T(8,128)S(1)} %fusion.57), channel_id=3, replica_groups=mesh['gx'=4,'gy'=8] {'gy'}, use_global_device_ids=true, to_apply=%region_6.8.clone | all-reduce | flops 8192 | bytes 65536
  155.2 1.9 fusion.3
  157.3 1.6 gather_fusion.6
  160.6 1.7 collective-permute-start.15
  165.0 3.2 %collective-permute-done.13 = f32[1,128,256]{2,1,0:T(8,128)S(1)} collective-permute-done((f32[1,128,256]{2,1,0:T(8,128)S(1)}, f32[1,128,256]{2,1,0:T(8,128)S(1)}, u32[]{:S(2)}, u32[]{:S(2)}) %collective-permute-start.13) | collective-permute-done | bytes 131104 | tf_op jit(solution)/shard_map/ppermute | solution.py:20
  168.3 1.6 gather_fusion.7
  169.9 4.0 %convolution_bitcast_fusion = f32[512,256]{0,1:T(8,128)} fusion(f32[1,1,512,512]{3,2,1,0:T(8,128)} %param.8, f32[512,256]{1,0:T(8,128)S(1)} %gather_fusion.7, pred[512]{0:T(512)(128)(4,1)S(1)} %compare_and_fusion), kind=kOutput, calls=%fused_computation.17 | convolution fusion | flops 805437440 | bytes 2097664 | tf_op jit(solution)/shard_map/dot_general | solution.py:28
  175.1 2.2 gather_fusion.8
  179.2 2.1 collective-permute-start.19
  182.4 2.0 collective-permute-done.16
  184.4 2.7 %collective-permute-done.17 = f32[1,128,256]{2,1,0:T(8,128)S(1)} collective-permute-done((f32[1,128,256]{2,1,0:T(8,128)S(1)}, f32[1,128,256]{2,1,0:T(8,128)S(1)}, u32[]{:S(2)}, u32[]{:S(2)}) %collective-permute-start.17) | collective-permute-done | bytes 131104 | tf_op jit(solution)/shard_map/ppermute | solution.py:20
  187.3 2.2 gather_fusion.9
  190.8 45.9 %all-reduce.2 = (f32[256]{0:T(256)S(1)}, f32[256]{0:T(256)S(1)}) all-reduce(f32[256]{0:T(256)S(1)} %get-tuple-element.4, f32[256]{0:T(256)S(1)} %get-tuple-element.3), channel_id=1, replica_groups=mesh['gx'=4,'gy'=8] {'gx','gy'}, use_global_device_ids=true, to_apply=%region_8.10 | all-reduce | flops 512 | bytes 4096 | tf_op jit(solution)/shard_map/psum | solution.py:76
  (90 shorter events, 27.0 us)
Async XLA Ops:
  0.6 47.8 %copy-start = (f32[1,1,512,512]{3,2,1,0:T(8,128)S(1)}, f32[1,1,512,512]{3,2,1,0:T(8,128)}, u32[]{:S(2)}) copy-start(f32[1,1,512,512]{3,2,1,0:T(8,128)} %param.9) | copy-start | bytes 3145732
  0.6 0.8 copy-start.2
  4.3 8.4 %collective-permute-start = (f32[1,128,256]{2,1,0:T(8,128)S(1)}, f32[1,128,256]{2,1,0:T(8,128)S(1)}, u32[]{:S(2)}, u32[]{:S(2)}) collective-permute-start(f32[1,128,256]{2,1,0:T(8,128)S(1)} %get-tuple-element.47), channel_id=1, source_target_pairs={{0,8},{8,16},{16,24},{24,0},{1,9},{9,17},{17,25},{25,1},{2,10},{10... | collective-permute-start | bytes 393224 | tf_op jit(solution)/shard_map/ppermute | solution.py:18
  5.8 6.8 %collective-permute-start.2 = (f32[1,128,256]{2,1,0:T(8,128)S(1)}, f32[1,128,256]{2,1,0:T(8,128)S(1)}, u32[]{:S(2)}, u32[]{:S(2)}) collective-permute-start(f32[1,128,256]{2,1,0:T(8,128)S(1)} %get-tuple-element.48), channel_id=1, source_target_pairs={{0,1},{1,2},{2,3},{3,4},{4,5},{5,6},{6,7},{7,0},{8,9},{9,10},{10,1... | collective-permute-start | bytes 393224 | tf_op jit(solution)/shard_map/ppermute | solution.py:18
  5.8 6.8 %collective-permute-start.3 = (f32[1,128,256]{2,1,0:T(8,128)S(1)}, f32[1,128,256]{2,1,0:T(8,128)S(1)}, u32[]{:S(2)}, u32[]{:S(2)}) collective-permute-start(f32[1,128,256]{2,1,0:T(8,128)S(1)} %get-tuple-element.49), channel_id=1, source_target_pairs={{1,0},{2,1},{3,2},{4,3},{5,4},{6,5},{7,6},{0,7},{9,8},{10,9},{11,1... | collective-permute-start | bytes 393224 | tf_op jit(solution)/shard_map/ppermute | solution.py:20
  7.6 6.2 %collective-permute-start.1 = (f32[1,128,256]{2,1,0:T(8,128)S(1)}, f32[1,128,256]{2,1,0:T(8,128)S(1)}, u32[]{:S(2)}, u32[]{:S(2)}) collective-permute-start(f32[1,128,256]{2,1,0:T(8,128)S(1)} %get-tuple-element.50), channel_id=1, source_target_pairs={{8,0},{16,8},{24,16},{0,24},{9,1},{17,9},{25,17},{1,25},{10,2},{18... | collective-permute-start | bytes 393224 | tf_op jit(solution)/shard_map/ppermute | solution.py:20
  8.1 2.5 %copy-start.3 = (f32[32,128]{1,0:T(8,128)S(1)}, f32[32,128]{1,0:T(8,128)}, u32[]{:S(2)}) copy-start(f32[32,128]{1,0:T(8,128)} %param.11) | copy-start | bytes 49156
  10.7 0.7 copy-start.5
  15.5 0.7 copy-start.4
  52.4 5.3 %collective-permute-start.4 = (f32[1,128,256]{2,1,0:T(8,128)S(1)}, f32[1,128,256]{2,1,0:T(8,128)S(1)}, u32[]{:S(2)}, u32[]{:S(2)}) collective-permute-start(f32[1,128,256]{2,1,0:T(8,128)S(1)} %get-tuple-element.39), channel_id=1, source_target_pairs={{0,8},{8,16},{16,24},{24,0},{1,9},{9,17},{17,25},{25,1},{2,10},{10... | collective-permute-start | bytes 393224 | tf_op jit(solution)/shard_map/ppermute | solution.py:18
  53.9 4.4 %collective-permute-start.6 = (f32[1,128,256]{2,1,0:T(8,128)S(1)}, f32[1,128,256]{2,1,0:T(8,128)S(1)}, u32[]{:S(2)}, u32[]{:S(2)}) collective-permute-start(f32[1,128,256]{2,1,0:T(8,128)S(1)} %get-tuple-element.40), channel_id=1, source_target_pairs={{0,1},{1,2},{2,3},{3,4},{4,5},{5,6},{6,7},{7,0},{8,9},{9,10},{10,1... | collective-permute-start | bytes 393224 | tf_op jit(solution)/shard_map/ppermute | solution.py:18
  53.9 4.4 %collective-permute-start.7 = (f32[1,128,256]{2,1,0:T(8,128)S(1)}, f32[1,128,256]{2,1,0:T(8,128)S(1)}, u32[]{:S(2)}, u32[]{:S(2)}) collective-permute-start(f32[1,128,256]{2,1,0:T(8,128)S(1)} %get-tuple-element.41), channel_id=1, source_target_pairs={{1,0},{2,1},{3,2},{4,3},{5,4},{6,5},{7,6},{0,7},{9,8},{10,9},{11,1... | collective-permute-start | bytes 393224 | tf_op jit(solution)/shard_map/ppermute | solution.py:20
  55.7 5.9 %collective-permute-start.5 = (f32[1,128,256]{2,1,0:T(8,128)S(1)}, f32[1,128,256]{2,1,0:T(8,128)S(1)}, u32[]{:S(2)}, u32[]{:S(2)}) collective-permute-start(f32[1,128,256]{2,1,0:T(8,128)S(1)} %get-tuple-element.42), channel_id=1, source_target_pairs={{8,0},{16,8},{24,16},{0,24},{9,1},{17,9},{25,17},{1,25},{10,2},{18... | collective-permute-start | bytes 393224 | tf_op jit(solution)/shard_map/ppermute | solution.py:20
  68.4 5.8 %collective-permute-start.8 = (f32[1,128,256]{2,1,0:T(8,128)S(1)}, f32[1,128,256]{2,1,0:T(8,128)S(1)}, u32[]{:S(2)}, u32[]{:S(2)}) collective-permute-start(f32[1,128,256]{2,1,0:T(8,128)S(1)} %get-tuple-element.31), channel_id=1, source_target_pairs={{0,8},{8,16},{16,24},{24,0},{1,9},{9,17},{17,25},{25,1},{2,10},{10... | collective-permute-start | bytes 393224 | tf_op jit(solution)/shard_map/ppermute | solution.py:18
  69.5 4.7 %collective-permute-start.10 = (f32[1,128,256]{2,1,0:T(8,128)S(1)}, f32[1,128,256]{2,1,0:T(8,128)S(1)}, u32[]{:S(2)}, u32[]{:S(2)}) collective-permute-start(f32[1,128,256]{2,1,0:T(8,128)S(1)} %get-tuple-element.32), channel_id=1, source_target_pairs={{0,1},{1,2},{2,3},{3,4},{4,5},{5,6},{6,7},{7,0},{8,9},{9,10},{10,1... | collective-permute-start | bytes 393224 | tf_op jit(solution)/shard_map/ppermute | solution.py:18
  69.5 4.7 %collective-permute-start.11 = (f32[1,128,256]{2,1,0:T(8,128)S(1)}, f32[1,128,256]{2,1,0:T(8,128)S(1)}, u32[]{:S(2)}, u32[]{:S(2)}) collective-permute-start(f32[1,128,256]{2,1,0:T(8,128)S(1)} %get-tuple-element.33), channel_id=1, source_target_pairs={{1,0},{2,1},{3,2},{4,3},{5,4},{6,5},{7,6},{0,7},{9,8},{10,9},{11,1... | collective-permute-start | bytes 393224 | tf_op jit(solution)/shard_map/ppermute | solution.py:20
  71.6 5.9 %collective-permute-start.9 = (f32[1,128,256]{2,1,0:T(8,128)S(1)}, f32[1,128,256]{2,1,0:T(8,128)S(1)}, u32[]{:S(2)}, u32[]{:S(2)}) collective-permute-start(f32[1,128,256]{2,1,0:T(8,128)S(1)} %get-tuple-element.34), channel_id=1, source_target_pairs={{8,0},{16,8},{24,16},{0,24},{9,1},{17,9},{25,17},{1,25},{10,2},{18... | collective-permute-start | bytes 393224 | tf_op jit(solution)/shard_map/ppermute | solution.py:20
  159.1 5.3 %collective-permute-start.12 = (f32[1,128,256]{2,1,0:T(8,128)S(1)}, f32[1,128,256]{2,1,0:T(8,128)S(1)}, u32[]{:S(2)}, u32[]{:S(2)}) collective-permute-start(f32[1,128,256]{2,1,0:T(8,128)S(1)} %get-tuple-element.23), channel_id=1, source_target_pairs={{0,8},{8,16},{16,24},{24,0},{1,9},{9,17},{17,25},{25,1},{2,10},{10... | collective-permute-start | bytes 393224 | tf_op jit(solution)/shard_map/ppermute | solution.py:18
  160.6 4.4 %collective-permute-start.14 = (f32[1,128,256]{2,1,0:T(8,128)S(1)}, f32[1,128,256]{2,1,0:T(8,128)S(1)}, u32[]{:S(2)}, u32[]{:S(2)}) collective-permute-start(f32[1,128,256]{2,1,0:T(8,128)S(1)} %get-tuple-element.24), channel_id=1, source_target_pairs={{0,1},{1,2},{2,3},{3,4},{4,5},{5,6},{6,7},{7,0},{8,9},{9,10},{10,1... | collective-permute-start | bytes 393224 | tf_op jit(solution)/shard_map/ppermute | solution.py:18
  160.6 4.4 %collective-permute-start.15 = (f32[1,128,256]{2,1,0:T(8,128)S(1)}, f32[1,128,256]{2,1,0:T(8,128)S(1)}, u32[]{:S(2)}, u32[]{:S(2)}) collective-permute-start(f32[1,128,256]{2,1,0:T(8,128)S(1)} %get-tuple-element.25), channel_id=1, source_target_pairs={{1,0},{2,1},{3,2},{4,3},{5,4},{6,5},{7,6},{0,7},{9,8},{10,9},{11,1... | collective-permute-start | bytes 393224 | tf_op jit(solution)/shard_map/ppermute | solution.py:20
  162.3 5.9 %collective-permute-start.13 = (f32[1,128,256]{2,1,0:T(8,128)S(1)}, f32[1,128,256]{2,1,0:T(8,128)S(1)}, u32[]{:S(2)}, u32[]{:S(2)}) collective-permute-start(f32[1,128,256]{2,1,0:T(8,128)S(1)} %get-tuple-element.26), channel_id=1, source_target_pairs={{8,0},{16,8},{24,16},{0,24},{9,1},{17,9},{25,17},{1,25},{10,2},{18... | collective-permute-start | bytes 393224 | tf_op jit(solution)/shard_map/ppermute | solution.py:20
  178.6 5.8 %collective-permute-start.16 = (f32[1,128,256]{2,1,0:T(8,128)S(1)}, f32[1,128,256]{2,1,0:T(8,128)S(1)}, u32[]{:S(2)}, u32[]{:S(2)}) collective-permute-start(f32[1,128,256]{2,1,0:T(8,128)S(1)} %get-tuple-element.15), channel_id=1, source_target_pairs={{0,8},{8,16},{16,24},{24,0},{1,9},{9,17},{17,25},{25,1},{2,10},{10... | collective-permute-start | bytes 393224 | tf_op jit(solution)/shard_map/ppermute | solution.py:18
  179.2 5.2 %collective-permute-start.18 = (f32[1,128,256]{2,1,0:T(8,128)S(1)}, f32[1,128,256]{2,1,0:T(8,128)S(1)}, u32[]{:S(2)}, u32[]{:S(2)}) collective-permute-start(f32[1,128,256]{2,1,0:T(8,128)S(1)} %get-tuple-element.16), channel_id=1, source_target_pairs={{0,1},{1,2},{2,3},{3,4},{4,5},{5,6},{6,7},{7,0},{8,9},{9,10},{10,1... | collective-permute-start | bytes 393224 | tf_op jit(solution)/shard_map/ppermute | solution.py:18
  179.2 5.2 %collective-permute-start.19 = (f32[1,128,256]{2,1,0:T(8,128)S(1)}, f32[1,128,256]{2,1,0:T(8,128)S(1)}, u32[]{:S(2)}, u32[]{:S(2)}) collective-permute-start(f32[1,128,256]{2,1,0:T(8,128)S(1)} %get-tuple-element.17), channel_id=1, source_target_pairs={{1,0},{2,1},{3,2},{4,3},{5,4},{6,5},{7,6},{0,7},{9,8},{10,9},{11,1... | collective-permute-start | bytes 393224 | tf_op jit(solution)/shard_map/ppermute | solution.py:20
  181.3 5.9 %collective-permute-start.17 = (f32[1,128,256]{2,1,0:T(8,128)S(1)}, f32[1,128,256]{2,1,0:T(8,128)S(1)}, u32[]{:S(2)}, u32[]{:S(2)}) collective-permute-start(f32[1,128,256]{2,1,0:T(8,128)S(1)} %get-tuple-element.18), channel_id=1, source_target_pairs={{8,0},{16,8},{24,16},{0,24},{9,1},{17,9},{25,17},{1,25},{10,2},{18... | collective-permute-start | bytes 393224 | tf_op jit(solution)/shard_map/ppermute | solution.py:20
  189.5 47.2 %copy-start.1 = (f32[512,256]{1,0:T(8,128)S(1)}, f32[512,256]{1,0:T(8,128)}, u32[]{:S(2)}) copy-start(f32[512,256]{1,0:T(8,128)} %gather_fusion.9) | copy-start | bytes 1572868
where the time goes:
time: 238 us
  blocking collectives  152 us (64%)
  local copies, waits for them, and re-layouts  24.6 us (10%)
  waiting for transfers between devices  21.7 us (9%)
  starting transfers between devices  19.1 us (8%)
  matrix products  13 us (5%)
  other arithmetic  5.91 us (2%)
    psum x2, blocking collectives, on_device(): numerator = lax.psum(jnp.sum(residual * search, axis=0), ('gx', 'gy'))  91.8 us
    unnamed x2, blocking collectives  45 us
    all_gather x2, blocking collectives, coarse_by_column(): column_res = lax.all_gather(corner_res, 'gx', axis=0, tiled=True)  15.1 us
    ppermute x10, waiting for transfers between devices, with_halo(): lax.ppermute(head, axis, [((i + 1) % count, i) for i in range(count)])  13.5 us
    dot_general x10, matrix products, matmul(): jnp.dot(first_op, second_op, precision=highest, preferred_element_type=jn...  13 us
    ppermute x10, starting transfers between devices, with_halo(): lax.ppermute(head, axis, [((i + 1) % count, i) for i in range(count)])  12.9 us
    gather x5, local copies, waits for them, and re-layouts, edge_jumps(): jnp.take(source, local_rows, axis=0).reshape(4, edge_size, source.shape[1])  9.57 us
    gather x5, local copies, waits for them, and re-layouts, edge_jumps(): return jnp.take(stacked, inverse, axis=0)  8.53 us
  transfers between devices with their start and end apart: 20, of which 11 were waited for; matrix products, arithmetic and copies ran while one was open for 1% of the time, Pallas kernels for 0%

commit v1 on v0

--- a/solution.py
+++ b/solution.py
@@ -44,7 +44,12 @@
 def coarse_by_column(corner_res, coarse_inv, grid_row):
     across_count = lax.axis_size("gx")
     along_count = lax.axis_size("gy")
-    column_res = lax.all_gather(corner_res, "gx", axis=0, tiled=True)
+    ring = [corner_res]
+    for hop in range(3):
+        ring.append(lax.ppermute(ring[-1], "gx", [(dev, (dev + 1) % 4) for dev in range(4)]))
+    column_res = jnp.roll(
+        jnp.concatenate(ring[::-1], axis=0), (lax.axis_index("gx") + 1) * ring[0].shape[0], axis=0
+    )
     group_rows = coarse_inv.shape[0]
     shaped = coarse_inv.reshape(group_rows, across_count, along_count, MODES)
     chosen = lax.dynamic_slice_in_dim(shaped, grid_row, 1, 2).reshape(

time: 238 us -> 251 us (1.055)
  blocking collectives: 152 us -> 138 us
  waiting for transfers between devices: 21.7 us -> 35.1 us
  starting transfers between devices: 19.1 us -> 32.4 us
    all_gather x2 -> x0, blocking collectives: 15.1 us -> none  [coarse_by_column(): column_res = lax.all_gather(corner_res, 'gx', axis=0, tiled=True)]
    ppermute x0 -> x6, starting transfers between devices: none -> 11.6 us  [coarse_by_column(): lax.ppermute(ring[-1], 'gx', [(dev, (dev + 1) % 4) for dev in range(4)])]
    ppermute x0 -> x6, waiting for transfers between devices: none -> 9.84 us  [coarse_by_column(): lax.ppermute(ring[-1], 'gx', [(dev, (dev + 1) % 4) for dev in range(4)])]
    ppermute x10, waiting for transfers between devices: 8.15 us -> 11.7 us  [with_halo(): lax.ppermute(tail, axis, [(i, (i + 1) % count) for i in range(count)])]
  transfers between devices with their start and end apart: 20 -> 26, of which waited for: 11 -> 19; matrix products, arithmetic and copies ran while one was open for 1% -> 0% of each run, Pallas kernels for 0% -> 0%
where the time goes in v1:
time: 251 us
  blocking collectives  138 us (55%)
  waiting for transfers between devices  35.1 us (14%)
  starting transfers between devices  32.4 us (13%)
  local copies, waits for them, and re-layouts  24.5 us (10%)
  matrix products  13 us (5%)
  other arithmetic  5.89 us (2%)
    psum x2, blocking collectives, on_device(): numerator = lax.psum(jnp.sum(residual * search, axis=0), ('gx', 'gy'))  93.4 us
    unnamed x2, blocking collectives  44.8 us
    ppermute x10, waiting for transfers between devices, with_halo(): lax.ppermute(head, axis, [((i + 1) % count, i) for i in range(count)])  13.6 us
    ppermute x10, starting transfers between devices, with_halo(): lax.ppermute(head, axis, [((i + 1) % count, i) for i in range(count)])  13.2 us
    dot_general x10, matrix products, matmul(): jnp.dot(first_op, second_op, precision=highest, preferred_element_type=jn...  13 us
    ppermute x10, waiting for transfers between devices, with_halo(): lax.ppermute(tail, axis, [(i, (i + 1) % count) for i in range(count)])  11.7 us
    ppermute x6, starting transfers between devices, coarse_by_column(): lax.ppermute(ring[-1], 'gx', [(dev, (dev + 1) % 4) for dev in range(4)])  11.6 us
    ppermute x6, waiting for transfers between devices, coarse_by_column(): lax.ppermute(ring[-1], 'gx', [(dev, (dev + 1) % 4) for dev in range(4)])  9.84 us
  transfers between devices with their start and end apart: 26, of which 19 were waited for; matrix products, arithmetic and copies ran while one was open for 0% of the time, Pallas kernels for 0%

profile of v1, /device:TPU:10, one launch (start us, length us, event | category | flops | bytes accessed | tf_op | source)
XLA Modules:
  0.0 250.8 jit_solution(9769121495454574540)
XLA Ops:
  1.4 2.4 scatter_custom_fusion
  3.9 2.6 %gather_fusion = f32[512,256]{1,0:T(8,128)S(1)} fusion(f32[512,256]{1,0:T(8,128)} %bitcast.130, s32[1024]{0:T(1024)S(1)} %pad_clamp_fusion.1), kind=kCustom, calls=%fused_computation.clone | custom fusion | bytes 1050624 | tf_op jit(solution)/shard_map/jit(_take)/gather | solution.py:33
  8.3 1.7 collective-permute-start.3
  13.8 2.4 collective-permute-done.1
  19.6 3.0 %collective-permute-done.4 = f32[4,256]{1,0:T(4,128)S(1)} collective-permute-done((f32[4,256]{1,0:T(4,128)S(1)}, f32[4,256]{1,0:T(4,128)S(1)}, u32[]{:S(2)}, u32[]{:S(2)}) %collective-permute-start.4) | collective-permute-done | bytes 4128 | tf_op jit(solution)/shard_map/ppermute | solution.py:49
  24.2 2.0 collective-permute-done.5
  26.2 2.4 collective-permute-start.6
  30.7 23.8 %all-reduce = f32[32,256]{1,0:T(8,128)S(1)} all-reduce(f32[32,256]{1,0:T(8,128)S(1)} %fusion.35), channel_id=2, replica_groups=mesh['gx'=4,'gy'=8] {'gy'}, use_global_device_ids=true, to_apply=%region_1.4.clone | all-reduce | flops 8192 | bytes 65536
  55.0 2.0 fusion.2
  58.9 2.7 %collective-permute-start.7 = (f32[1,128,256]{2,1,0:T(8,128)S(1)}, f32[1,128,256]{2,1,0:T(8,128)S(1)}, u32[]{:S(2)}, u32[]{:S(2)}) collective-permute-start(f32[1,128,256]{2,1,0:T(8,128)S(1)} %get-tuple-element.40), channel_id=1, source_target_pairs={{0,8},{8,16},{16,24},{24,0},{1,9},{9,17},{17,25},{25,1},{2,10},{10... | collective-permute-start | bytes 393224 | tf_op jit(solution)/shard_map/ppermute | solution.py:18
  63.3 2.0 collective-permute-done.7
  66.0 3.2 %collective-permute-done.8 = f32[1,128,256]{2,1,0:T(8,128)S(1)} collective-permute-done((f32[1,128,256]{2,1,0:T(8,128)S(1)}, f32[1,128,256]{2,1,0:T(8,128)S(1)}, u32[]{:S(2)}, u32[]{:S(2)}) %collective-permute-start.8) | collective-permute-done | bytes 131104 | tf_op jit(solution)/shard_map/ppermute | solution.py:20
  70.9 3.2 %convolution_bitcast_fusion.1 = f32[512,256]{0,1:T(8,128)S(1)} fusion(f32[1,1,512,512]{3,2,1,0:T(8,128)} %param.10, f32[512,256]{1,0:T(8,128)S(1)} %gather_fusion.3, pred[512]{0:T(512)(128)(4,1)S(1)} %get-tuple-element.56), kind=kOutput, calls=%fused_computation.18 | convolution fusion | flops 805437440 | bytes 2097664 | tf_op jit(solution)/shard_map/dot_general | solution.py:28
  76.2 1.8 collective-permute-start.14
  78.0 1.9 collective-permute-start.12
  79.9 2.2 collective-permute-done.11
  82.1 1.8 collective-permute-done.12
  85.7 46.7 %all-reduce.3 = (f32[256]{0:T(256)S(1)}, f32[256]{0:T(256)S(1)}) all-reduce(f32[256]{0:T(256)S(1)} %get-tuple-element.7, f32[256]{0:T(256)S(1)} %get-tuple-element.6), channel_id=1, replica_groups=mesh['gx'=4,'gy'=8] {'gx','gy'}, use_global_device_ids=true, to_apply=%region_3.6 | all-reduce | flops 512 | bytes 4096 | tf_op jit(solution)/shard_map/psum | solution.py:81
  134.4 2.2 collective-permute-done.15
  136.5 2.4 collective-permute-start.16
  140.2 3.2 %collective-permute-start.17 = (f32[4,256]{1,0:T(4,128)S(1)}, f32[4,256]{1,0:T(4,128)S(1)}, u32[]{:S(2)}, u32[]{:S(2)}) collective-permute-start(f32[4,256]{1,0:T(4,128)S(1)} %collective-permute-done.16), channel_id=1, source_target_pairs={{0,8},{8,16},{16,24},{24,0},{1,9},{9,17},{17,25},{25,1},{2,10},{10... | collective-permute-start | bytes 12296 | tf_op jit(solution)/shard_map/ppermute | solution.py:49
  144.9 21.0 %all-reduce.1 = f32[32,256]{1,0:T(8,128)S(1)} all-reduce(f32[32,256]{1,0:T(8,128)S(1)} %fusion.25), channel_id=3, replica_groups=mesh['gx'=4,'gy'=8] {'gy'}, use_global_device_ids=true, to_apply=%region_6.9.clone | all-reduce | flops 8192 | bytes 65536
  166.4 1.9 fusion.3
  170.3 3.2 %collective-permute-start.18 = (f32[1,128,256]{2,1,0:T(8,128)S(1)}, f32[1,128,256]{2,1,0:T(8,128)S(1)}, u32[]{:S(2)}, u32[]{:S(2)}) collective-permute-start(f32[1,128,256]{2,1,0:T(8,128)S(1)} %get-tuple-element.24), channel_id=1, source_target_pairs={{0,8},{8,16},{16,24},{24,0},{1,9},{9,17},{17,25},{25,1},{2,10},{10... | collective-permute-start | bytes 393224 | tf_op jit(solution)/shard_map/ppermute | solution.py:18
  175.2 2.0 collective-permute-done.18
  177.9 3.2 %collective-permute-done.19 = f32[1,128,256]{2,1,0:T(8,128)S(1)} collective-permute-done((f32[1,128,256]{2,1,0:T(8,128)S(1)}, f32[1,128,256]{2,1,0:T(8,128)S(1)}, u32[]{:S(2)}, u32[]{:S(2)}) %collective-permute-start.19) | collective-permute-done | bytes 131104 | tf_op jit(solution)/shard_map/ppermute | solution.py:20
  182.8 4.0 %convolution_bitcast_fusion = f32[512,256]{0,1:T(8,128)} fusion(f32[1,1,512,512]{3,2,1,0:T(8,128)} %param.10, f32[512,256]{1,0:T(8,128)S(1)} %gather_fusion.7, pred[512]{0:T(512)(128)(4,1)S(1)} %get-tuple-element.56), kind=kOutput, calls=%fused_computation.17 | convolution fusion | flops 805437440 | bytes 2097664 | tf_op jit(solution)/shard_map/dot_general | solution.py:28
  188.0 2.2 gather_fusion.8
  193.3 2.0 collective-permute-start.23
  195.3 2.2 collective-permute-done.22
  199.3 2.2 gather_fusion.9
  202.9 46.7 %all-reduce.2 = (f32[256]{0:T(256)S(1)}, f32[256]{0:T(256)S(1)}) all-reduce(f32[256]{0:T(256)S(1)} %get-tuple-element.5, f32[256]{0:T(256)S(1)} %get-tuple-element.4), channel_id=1, replica_groups=mesh['gx'=4,'gy'=8] {'gx','gy'}, use_global_device_ids=true, to_apply=%region_8.11 | all-reduce | flops 512 | bytes 4096 | tf_op jit(solution)/shard_map/psum | solution.py:81
  (96 shorter events, 43.1 us)
Async XLA Ops:
  0.6 54.4 %copy-start = (f32[1,1,512,512]{3,2,1,0:T(8,128)S(1)}, f32[1,1,512,512]{3,2,1,0:T(8,128)}, u32[]{:S(2)}) copy-start(f32[1,1,512,512]{3,2,1,0:T(8,128)} %param.11) | copy-start | bytes 3145732
  1.4 2.4 copy-start.2
  6.7 5.3 %collective-permute-start = (f32[1,128,256]{2,1,0:T(8,128)S(1)}, f32[1,128,256]{2,1,0:T(8,128)S(1)}, u32[]{:S(2)}, u32[]{:S(2)}) collective-permute-start(f32[1,128,256]{2,1,0:T(8,128)S(1)} %get-tuple-element.48), channel_id=1, source_target_pairs={{0,8},{8,16},{16,24},{24,0},{1,9},{9,17},{17,25},{25,1},{2,10},{10... | collective-permute-start | bytes 393224 | tf_op jit(solution)/shard_map/ppermute | solution.py:18
  8.3 4.4 %collective-permute-start.2 = (f32[1,128,256]{2,1,0:T(8,128)S(1)}, f32[1,128,256]{2,1,0:T(8,128)S(1)}, u32[]{:S(2)}, u32[]{:S(2)}) collective-permute-start(f32[1,128,256]{2,1,0:T(8,128)S(1)} %get-tuple-element.49), channel_id=1, source_target_pairs={{0,1},{1,2},{2,3},{3,4},{4,5},{5,6},{6,7},{7,0},{8,9},{9,10},{10,1... | collective-permute-start | bytes 393224 | tf_op jit(solution)/shard_map/ppermute | solution.py:18
  8.3 5.6 %collective-permute-start.3 = (f32[1,128,256]{2,1,0:T(8,128)S(1)}, f32[1,128,256]{2,1,0:T(8,128)S(1)}, u32[]{:S(2)}, u32[]{:S(2)}) collective-permute-start(f32[1,128,256]{2,1,0:T(8,128)S(1)} %get-tuple-element.50), channel_id=1, source_target_pairs={{1,0},{2,1},{3,2},{4,3},{5,4},{6,5},{7,6},{0,7},{9,8},{10,9},{11,1... | collective-permute-start | bytes 393224 | tf_op jit(solution)/shard_map/ppermute | solution.py:20
  10.0 6.2 %collective-permute-start.1 = (f32[1,128,256]{2,1,0:T(8,128)S(1)}, f32[1,128,256]{2,1,0:T(8,128)S(1)}, u32[]{:S(2)}, u32[]{:S(2)}) collective-permute-start(f32[1,128,256]{2,1,0:T(8,128)S(1)} %get-tuple-element.51), channel_id=1, source_target_pairs={{8,0},{16,8},{24,16},{0,24},{9,1},{17,9},{25,17},{1,25},{10,2},{18... | collective-permute-start | bytes 393224 | tf_op jit(solution)/shard_map/ppermute | solution.py:20
  18.0 0.7 copy-start.4
  18.6 5.5 %copy-start.3 = (f32[32,128]{1,0:T(8,128)S(1)}, f32[32,128]{1,0:T(8,128)}, u32[]{:S(2)}) copy-start(f32[32,128]{1,0:T(8,128)} %param.13) | copy-start | bytes 49156
  19.0 3.7 %collective-permute-start.4 = (f32[4,256]{1,0:T(4,128)S(1)}, f32[4,256]{1,0:T(4,128)S(1)}, u32[]{:S(2)}, u32[]{:S(2)}) collective-permute-start(f32[4,256]{1,0:T(4,128)S(1)} %fusion.10), channel_id=1, source_target_pairs={{0,8},{8,16},{16,24},{24,0},{1,9},{9,17},{17,25},{25,1},{2,10},{10... | collective-permute-start | bytes 12296 | tf_op jit(solution)/shard_map/ppermute | solution.py:49
  22.6 3.6 %collective-permute-start.5 = (f32[4,256]{1,0:T(4,128)S(1)}, f32[4,256]{1,0:T(4,128)S(1)}, u32[]{:S(2)}, u32[]{:S(2)}) collective-permute-start(f32[4,256]{1,0:T(4,128)S(1)} %collective-permute-done.4), channel_id=1, source_target_pairs={{0,8},{8,16},{16,24},{24,0},{1,9},{9,17},{17,25},{25,1},{2,10},{10... | collective-permute-start | bytes 12296 | tf_op jit(solution)/shard_map/ppermute | solution.py:49
  26.2 4.3 %collective-permute-start.6 = (f32[4,256]{1,0:T(4,128)S(1)}, f32[4,256]{1,0:T(4,128)S(1)}, u32[]{:S(2)}, u32[]{:S(2)}) collective-permute-start(f32[4,256]{1,0:T(4,128)S(1)} %collective-permute-done.5), channel_id=1, source_target_pairs={{0,8},{8,16},{16,24},{24,0},{1,9},{9,17},{17,25},{25,1},{2,10},{10... | collective-permute-start | bytes 12296 | tf_op jit(solution)/shard_map/ppermute | solution.py:49
  28.6 0.7 copy-start.5
  58.9 6.4 %collective-permute-start.7 = (f32[1,128,256]{2,1,0:T(8,128)S(1)}, f32[1,128,256]{2,1,0:T(8,128)S(1)}, u32[]{:S(2)}, u32[]{:S(2)}) collective-permute-start(f32[1,128,256]{2,1,0:T(8,128)S(1)} %get-tuple-element.40), channel_id=1, source_target_pairs={{0,8},{8,16},{16,24},{24,0},{1,9},{9,17},{17,25},{25,1},{2,10},{10... | collective-permute-start | bytes 393224 | tf_op jit(solution)/shard_map/ppermute | solution.py:18
  61.6 4.4 %collective-permute-start.9 = (f32[1,128,256]{2,1,0:T(8,128)S(1)}, f32[1,128,256]{2,1,0:T(8,128)S(1)}, u32[]{:S(2)}, u32[]{:S(2)}) collective-permute-start(f32[1,128,256]{2,1,0:T(8,128)S(1)} %get-tuple-element.41), channel_id=1, source_target_pairs={{0,1},{1,2},{2,3},{3,4},{4,5},{5,6},{6,7},{7,0},{8,9},{9,10},{10,1... | collective-permute-start | bytes 393224 | tf_op jit(solution)/shard_map/ppermute | solution.py:18
  61.6 4.4 %collective-permute-start.10 = (f32[1,128,256]{2,1,0:T(8,128)S(1)}, f32[1,128,256]{2,1,0:T(8,128)S(1)}, u32[]{:S(2)}, u32[]{:S(2)}) collective-permute-start(f32[1,128,256]{2,1,0:T(8,128)S(1)} %get-tuple-element.42), channel_id=1, source_target_pairs={{1,0},{2,1},{3,2},{4,3},{5,4},{6,5},{7,6},{0,7},{9,8},{10,9},{11,1... | collective-permute-start | bytes 393224 | tf_op jit(solution)/shard_map/ppermute | solution.py:20
  63.3 5.9 %collective-permute-start.8 = (f32[1,128,256]{2,1,0:T(8,128)S(1)}, f32[1,128,256]{2,1,0:T(8,128)S(1)}, u32[]{:S(2)}, u32[]{:S(2)}) collective-permute-start(f32[1,128,256]{2,1,0:T(8,128)S(1)} %get-tuple-element.43), channel_id=1, source_target_pairs={{8,0},{16,8},{24,16},{0,24},{9,1},{17,9},{25,17},{1,25},{10,2},{18... | collective-permute-start | bytes 393224 | tf_op jit(solution)/shard_map/ppermute | solution.py:20
  76.1 6.0 %collective-permute-start.11 = (f32[1,128,256]{2,1,0:T(8,128)S(1)}, f32[1,128,256]{2,1,0:T(8,128)S(1)}, u32[]{:S(2)}, u32[]{:S(2)}) collective-permute-start(f32[1,128,256]{2,1,0:T(8,128)S(1)} %get-tuple-element.32), channel_id=1, source_target_pairs={{0,8},{8,16},{16,24},{24,0},{1,9},{9,17},{17,25},{25,1},{2,10},{10... | collective-permute-start | bytes 393224 | tf_op jit(solution)/shard_map/ppermute | solution.py:18
  76.1 5.9 %collective-permute-start.13 = (f32[1,128,256]{2,1,0:T(8,128)S(1)}, f32[1,128,256]{2,1,0:T(8,128)S(1)}, u32[]{:S(2)}, u32[]{:S(2)}) collective-permute-start(f32[1,128,256]{2,1,0:T(8,128)S(1)} %get-tuple-element.33), channel_id=1, source_target_pairs={{0,1},{1,2},{2,3},{3,4},{4,5},{5,6},{6,7},{7,0},{8,9},{9,10},{10,1... | collective-permute-start | bytes 393224 | tf_op jit(solution)/shard_map/ppermute | solution.py:18
  76.2 5.9 %collective-permute-start.14 = (f32[1,128,256]{2,1,0:T(8,128)S(1)}, f32[1,128,256]{2,1,0:T(8,128)S(1)}, u32[]{:S(2)}, u32[]{:S(2)}) collective-permute-start(f32[1,128,256]{2,1,0:T(8,128)S(1)} %get-tuple-element.34), channel_id=1, source_target_pairs={{1,0},{2,1},{3,2},{4,3},{5,4},{6,5},{7,6},{0,7},{9,8},{10,9},{11,1... | collective-permute-start | bytes 393224 | tf_op jit(solution)/shard_map/ppermute | solution.py:20
  78.0 5.9 %collective-permute-start.12 = (f32[1,128,256]{2,1,0:T(8,128)S(1)}, f32[1,128,256]{2,1,0:T(8,128)S(1)}, u32[]{:S(2)}, u32[]{:S(2)}) collective-permute-start(f32[1,128,256]{2,1,0:T(8,128)S(1)} %get-tuple-element.35), channel_id=1, source_target_pairs={{8,0},{16,8},{24,16},{0,24},{9,1},{17,9},{25,17},{1,25},{10,2},{18... | collective-permute-start | bytes 393224 | tf_op jit(solution)/shard_map/ppermute | solution.py:20
  132.8 3.7 %collective-permute-start.15 = (f32[4,256]{1,0:T(4,128)S(1)}, f32[4,256]{1,0:T(4,128)S(1)}, u32[]{:S(2)}, u32[]{:S(2)}) collective-permute-start(f32[4,256]{1,0:T(4,128)S(1)} %fusion.42), channel_id=1, source_target_pairs={{0,8},{8,16},{16,24},{24,0},{1,9},{9,17},{17,25},{25,1},{2,10},{10... | collective-permute-start | bytes 12296 | tf_op jit(solution)/shard_map/ppermute | solution.py:49
  136.5 3.7 %collective-permute-start.16 = (f32[4,256]{1,0:T(4,128)S(1)}, f32[4,256]{1,0:T(4,128)S(1)}, u32[]{:S(2)}, u32[]{:S(2)}) collective-permute-start(f32[4,256]{1,0:T(4,128)S(1)} %collective-permute-done.15), channel_id=1, source_target_pairs={{0,8},{8,16},{16,24},{24,0},{1,9},{9,17},{17,25},{25,1},{2,10},{10... | collective-permute-start | bytes 12296 | tf_op jit(solution)/shard_map/ppermute | solution.py:49
  140.2 4.5 %collective-permute-start.17 = (f32[4,256]{1,0:T(4,128)S(1)}, f32[4,256]{1,0:T(4,128)S(1)}, u32[]{:S(2)}, u32[]{:S(2)}) collective-permute-start(f32[4,256]{1,0:T(4,128)S(1)} %collective-permute-done.16), channel_id=1, source_target_pairs={{0,8},{8,16},{16,24},{24,0},{1,9},{9,17},{17,25},{25,1},{2,10},{10... | collective-permute-start | bytes 12296 | tf_op jit(solution)/shard_map/ppermute | solution.py:49
  170.3 6.9 %collective-permute-start.18 = (f32[1,128,256]{2,1,0:T(8,128)S(1)}, f32[1,128,256]{2,1,0:T(8,128)S(1)}, u32[]{:S(2)}, u32[]{:S(2)}) collective-permute-start(f32[1,128,256]{2,1,0:T(8,128)S(1)} %get-tuple-element.24), channel_id=1, source_target_pairs={{0,8},{8,16},{16,24},{24,0},{1,9},{9,17},{17,25},{25,1},{2,10},{10... | collective-permute-start | bytes 393224 | tf_op jit(solution)/shard_map/ppermute | solution.py:18
  173.5 4.4 %collective-permute-start.20 = (f32[1,128,256]{2,1,0:T(8,128)S(1)}, f32[1,128,256]{2,1,0:T(8,128)S(1)}, u32[]{:S(2)}, u32[]{:S(2)}) collective-permute-start(f32[1,128,256]{2,1,0:T(8,128)S(1)} %get-tuple-element.25), channel_id=1, source_target_pairs={{0,1},{1,2},{2,3},{3,4},{4,5},{5,6},{6,7},{7,0},{8,9},{9,10},{10,1... | collective-permute-start | bytes 393224 | tf_op jit(solution)/shard_map/ppermute | solution.py:18
  173.5 4.4 %collective-permute-start.21 = (f32[1,128,256]{2,1,0:T(8,128)S(1)}, f32[1,128,256]{2,1,0:T(8,128)S(1)}, u32[]{:S(2)}, u32[]{:S(2)}) collective-permute-start(f32[1,128,256]{2,1,0:T(8,128)S(1)} %get-tuple-element.26), channel_id=1, source_target_pairs={{1,0},{2,1},{3,2},{4,3},{5,4},{6,5},{7,6},{0,7},{9,8},{10,9},{11,1... | collective-permute-start | bytes 393224 | tf_op jit(solution)/shard_map/ppermute | solution.py:20
  175.2 5.9 %collective-permute-start.19 = (f32[1,128,256]{2,1,0:T(8,128)S(1)}, f32[1,128,256]{2,1,0:T(8,128)S(1)}, u32[]{:S(2)}, u32[]{:S(2)}) collective-permute-start(f32[1,128,256]{2,1,0:T(8,128)S(1)} %get-tuple-element.27), channel_id=1, source_target_pairs={{8,0},{16,8},{24,16},{0,24},{9,1},{17,9},{25,17},{1,25},{10,2},{18... | collective-permute-start | bytes 393224 | tf_op jit(solution)/shard_map/ppermute | solution.py:20
  191.5 6.0 %collective-permute-start.22 = (f32[1,128,256]{2,1,0:T(8,128)S(1)}, f32[1,128,256]{2,1,0:T(8,128)S(1)}, u32[]{:S(2)}, u32[]{:S(2)}) collective-permute-start(f32[1,128,256]{2,1,0:T(8,128)S(1)} %get-tuple-element.16), channel_id=1, source_target_pairs={{0,8},{8,16},{16,24},{24,0},{1,9},{9,17},{17,25},{25,1},{2,10},{10... | collective-permute-start | bytes 393224 | tf_op jit(solution)/shard_map/ppermute | solution.py:18
  191.5 5.9 %collective-permute-start.24 = (f32[1,128,256]{2,1,0:T(8,128)S(1)}, f32[1,128,256]{2,1,0:T(8,128)S(1)}, u32[]{:S(2)}, u32[]{:S(2)}) collective-permute-start(f32[1,128,256]{2,1,0:T(8,128)S(1)} %get-tuple-element.17), channel_id=1, source_target_pairs={{0,1},{1,2},{2,3},{3,4},{4,5},{5,6},{6,7},{7,0},{8,9},{9,10},{10,1... | collective-permute-start | bytes 393224 | tf_op jit(solution)/shard_map/ppermute | solution.py:18
  191.6 5.9 %collective-permute-start.25 = (f32[1,128,256]{2,1,0:T(8,128)S(1)}, f32[1,128,256]{2,1,0:T(8,128)S(1)}, u32[]{:S(2)}, u32[]{:S(2)}) collective-permute-start(f32[1,128,256]{2,1,0:T(8,128)S(1)} %get-tuple-element.18), channel_id=1, source_target_pairs={{1,0},{2,1},{3,2},{4,3},{5,4},{6,5},{7,6},{0,7},{9,8},{10,9},{11,1... | collective-permute-start | bytes 393224 | tf_op jit(solution)/shard_map/ppermute | solution.py:20
  193.3 5.9 %collective-permute-start.23 = (f32[1,128,256]{2,1,0:T(8,128)S(1)}, f32[1,128,256]{2,1,0:T(8,128)S(1)}, u32[]{:S(2)}, u32[]{:S(2)}) collective-permute-start(f32[1,128,256]{2,1,0:T(8,128)S(1)} %get-tuple-element.19), channel_id=1, source_target_pairs={{8,0},{16,8},{24,16},{0,24},{9,1},{17,9},{25,17},{1,25},{10,2},{18... | collective-permute-start | bytes 393224 | tf_op jit(solution)/shard_map/ppermute | solution.py:20
  201.6 48.0 %copy-start.1 = (f32[512,256]{1,0:T(8,128)S(1)}, f32[512,256]{1,0:T(8,128)}, u32[]{:S(2)}) copy-start(f32[512,256]{1,0:T(8,128)} %gather_fusion.9) | copy-start | bytes 1572868
